TPU v7x, 128 devices: a whole 4x4x4 slice. The times are simulated.
128 devices in a mesh: wide: 32 (over z, y_hi, x), narrow: 4 (over y_lo, core).
Axes of the slice: x: 4, y: 4 (y_hi: 2, y_lo: 2; y = y_hi * 2 + y_lo), z: 4, core: 2. Of those that a mesh axis runs over, the one named last changes fastest.
Arguments:
- spectra: bfloat16 [2, 128, 64, 32, 256], P(None, ('wide', 'narrow')), may hold values from -6 to 6
- out_grads: bfloat16 [2, 128, 64, 32, 256], P(None, ('wide', 'narrow')), may hold values from -0.375 to 0.375
- weights: float32 [2, 64, 32, 256, 256], P(None, 'wide', 'narrow'), may hold values from -6 to 6
- mode_factor: float32 [64, 8], replicated, may hold values from -2 to 2
- in_factor: float32 [256, 64], replicated, may hold values from -0.75 to 0.75
- out_factor: float32 [256, 64], replicated, may hold values from -0.75 to 0.75
- first_moment: float32 [2, 8, 32, 4096], P(None, None, 'narrow', 'wide'), may hold values from -60 to 60
- second_moment: float32 [8, 32, 4096], P(None, 'narrow', 'wide'), may hold values from 20 to 500
Outputs:
- new_weights: float32 [2, 64, 32, 256, 256], P(None, 'wide', 'narrow')
- new_first: float32 [2, 8, 32, 4096], P(None, None, 'narrow', 'wide')
- new_second: float32 [8, 32, 4096], P(None, 'narrow', 'wide')
All inputs are finite; a program needn't handle non-finite values.
Results may differ from a plain program's by a relative error of at most 0.0003.
Values may be sent and summed in bfloat16 or wider, within the bound.
No kernel may reach another device: no remote copies, remote signals or barrier semaphores. Data moves between devices by JAX's collectives and lax.ppermute only.
A program may use at most 128 MiB of HBM per device.

v0:
```python
import jax
import jax.numpy as jnp
from jax import lax
from jax.sharding import PartitionSpec as P

STEP = 1000


highest = lax.Precision.HIGHEST


def local(
    spectra, out_grads, weights, mode_factor, in_factor, out_factor, first_moment, second_moment
):
    wide_count = lax.axis_size("wide")
    narrow_count = lax.axis_size("narrow")
    modes_first = spectra.shape[2]
    modes_second = spectra.shape[3]
    channels = spectra.shape[4]
    first_mine = modes_first // wide_count
    second_mine = modes_second // narrow_count
    local_modes = first_mine * second_mine
    rank_in = in_factor.shape[1]
    rank_out = out_factor.shape[1]

    def arrange(source):
        sample_rows = source.shape[1]
        width = source.shape[4]
        source = source.reshape(
            2, sample_rows, wide_count, first_mine, narrow_count, second_mine, width
        )
        source = source.transpose(0, 1, 2, 4, 3, 5, 6)
        return source.reshape(2, sample_rows, wide_count * narrow_count * local_modes, width)

    mine_spectra, mine_grads = (
        lax.all_to_all(
            arrange(spectra), ("wide", "narrow"), split_axis=2, concat_axis=1, tiled=True
        ),
        lax.all_to_all(
            arrange(out_grads), ("wide", "narrow"), split_axis=2, concat_axis=1, tiled=True
        ),
    )
    products = jnp.einsum(
        "pbmi,qbmo->pqmio", mine_spectra, mine_grads, preferred_element_type=jnp.float32
    )
    grad = jnp.stack([products[0, 0] + products[1, 1], products[0, 1] - products[1, 0]])
    half_core = jnp.einsum("pmio,oc->pmic", grad, out_factor, precision=highest)
    channel_core = jnp.einsum("ia,pmic->pmac", in_factor, half_core, precision=highest)
    channel_core = channel_core.reshape(2, first_mine, second_mine, rank_in * rank_out)
    wide_position = lax.axis_index("wide")
    mine_rows = lax.dynamic_slice_in_dim(mode_factor, wide_position * first_mine, first_mine, 0)
    partial_core = jnp.einsum("xr,pxmk->prmk", mine_rows, channel_core, precision=highest)
    core_grad = lax.psum_scatter(partial_core, "wide", scatter_dimension=3, tiled=True)
    new_first = 0.9 * first_moment + 0.1 * core_grad
    new_second = 0.999 * second_moment + 0.001 * (
        core_grad[0] * core_grad[0] + core_grad[1] * core_grad[1]
    )
    first_scale = 1.0 / (1.0 - 0.9**STEP)
    second_scale = 1.0 / (1.0 - 0.999**STEP)
    core_step = new_first * first_scale / (jnp.sqrt(new_second * second_scale) + 1e-08)
    expanded = jnp.einsum(
        "xr,prmk->pxmk",
        mine_rows,
        lax.all_gather(core_step, "wide", axis=3, tiled=True),
        precision=highest,
    )
    expanded = expanded.reshape(2, local_modes, rank_in, rank_out)
    left_part = jnp.einsum("pmac,oc->pmao", expanded, out_factor, precision=highest)
    change = jnp.einsum("ia,pmao->pmio", in_factor, left_part, precision=highest)
    change = change.reshape(2, first_mine, second_mine, channels, channels)
    new_weights = weights - 0.3 * change
    return (new_weights, new_first, new_second)


def solution(mesh):
    placed = (
        P(None, ("wide", "narrow"), None, None, None),
        P(None, ("wide", "narrow"), None, None, None),
        P(None, "wide", "narrow", None, None),
        P(),
        P(),
        P(),
        P(None, None, "narrow", "wide"),
        P(None, "narrow", "wide"),
    )
    return jax.shard_map(
        local,
        mesh=mesh,
        in_specs=placed,
        out_specs=(
            P(None, "wide", "narrow", None, None),
            P(None, None, "narrow", "wide"),
            P(None, "narrow", "wide"),
        ),
        check_vma=False,
    )
```

profile of v0, /device:TPU:0, one launch (start us, length us, event | category | flops | bytes accessed | tf_op | source)
XLA Modules:
  0.0 412.7 jit_solution(15778321747352976225)
XLA Ops:
  7.2 1.8 copy.52
  9.0 14.0 %copy.53 = bf16[2,1,2048,256]{3,0,1,2:T(2,128)(2,1)} copy(bf16[2,1,2048,256]{3,2,0,1:T(8,128)(2,1)S(1)} %bitcast.77) | data formatting | bytes 4194304 | tf_op jit(solution)/shard_map/reshape | solution.py:33
  23.0 11.2 %all-to-all-start.1 = ((bf16[2,1,2048,256]{3,0,1,2:T(2,128)(2,1)}), bf16[2,1,2048,256]{3,0,1,2:T(2,128)(2,1)S(1)}, u32[]{:S(2)}, u32[]{:S(2)}) async-start(bf16[2,1,2048,256]{3,0,1,2:T(2,128)(2,1)} %copy.53), calls=%async_computation.1 | async-start | bytes 4194304 | tf_op jit(solution)/shard_map/all_to_all | solution.py:36
  34.2 1.8 copy.49
  36.0 14.0 %copy.50 = bf16[2,1,2048,256]{3,0,1,2:T(2,128)(2,1)} copy(bf16[2,1,2048,256]{3,2,0,1:T(8,128)(2,1)S(1)} %bitcast.78) | data formatting | bytes 4194304 | tf_op jit(solution)/shard_map/reshape | solution.py:33
  49.9 14.4 %all-to-all-done.1 = bf16[2,1,2048,256]{3,0,1,2:T(2,128)(2,1)S(1)} async-done(((bf16[2,1,2048,256]{3,0,1,2:T(2,128)(2,1)}), bf16[2,1,2048,256]{3,0,1,2:T(2,128)(2,1)S(1)}, u32[]{:S(2)}, u32[]{:S(2)}) %all-to-all-start.1) | async-done | bytes 2097184 | tf_op jit(solution)/shard_map/all_to_all | solution.py:36
  64.3 5.8 %all-to-all-start = ((bf16[2,1,2048,256]{3,0,1,2:T(2,128)(2,1)}), bf16[2,1,2048,256]{3,0,1,2:T(2,128)(2,1)}, u32[]{:S(2)}, u32[]{:S(2)}) async-start(bf16[2,1,2048,256]{3,0,1,2:T(2,128)(2,1)} %copy.50), calls=%async_computation | async-start | bytes 4194304 | tf_op jit(solution)/shard_map/all_to_all | solution.py:39
  70.1 0.2 reduce-scatter.2.cloned.1.call-start
  70.3 29.5 %all-to-all-done = bf16[2,1,2048,256]{3,0,1,2:T(2,128)(2,1)} async-done(((bf16[2,1,2048,256]{3,0,1,2:T(2,128)(2,1)}), bf16[2,1,2048,256]{3,0,1,2:T(2,128)(2,1)}, u32[]{:S(2)}, u32[]{:S(2)}) %all-to-all-start) | async-done | bytes 2097184 | tf_op jit(solution)/shard_map/all_to_all | solution.py:39
  99.8 7.4 %convolution_bitcast_fusion = f32[2,2,16,256,256]{3,4,0,1,2:T(8,128)S(1)} fusion(bf16[2,128,16,256,1]{3,0,2,1,4:T(2,128)(2,1)S(1)} %bitcast.76, bf16[2,128,16,256,1]{3,0,2,1,4:T(2,128)(2,1)} %bitcast.4), kind=kOutput, calls=%fused_computation | convolution fusion | flops 1073741824 | bytes 20971520 | tf_op jit(solution)/shard_map/pbmi,qbmo->pqmio/dot_general | solution.py:43
  107.2 0.6 fusion.4
  107.8 0.6 fusion.6
  108.4 0.2 copy-done.1
  108.6 5.6 %fusion = f32[2,16,256,64]{2,3,1,0:T(8,128)S(1)} fusion(f32[1,16,256,256]{2,3,1,0:T(8,128)S(1)} %fusion.4, f32[1,16,256,256]{2,3,1,0:T(8,128)S(1)} %fusion.6, f32[256,64]{0,1:T(8,128)S(1)} %copy-done.1), kind=kOutput, calls=%fused_computation.1 | convolution fusion | flops 1612709888 | bytes 10551296 | tf_op jit(solution)/shard_map/pmio,oc->pmic/dot_general | solution.py:47
  114.2 2.0 convolution_bitcast_fusion.3
  116.3 0.3 copy.60
  116.6 0.4 reshape.79
  117.0 3.5 convolution_bitcast_fusion.1
  120.6 0.0 all-gather.2.cloned.1.call-start
  120.6 185.0 %reduce-scatter.2.cloned.1.call-done = f32[2,8,8,128]{3,1,2,0:T(8,128)} async-done(((f32[2,8,8,4096]{3,1,2,0:T(8,128)}), f32[2,8,8,128]{3,1,2,0:T(8,128)}) %reduce-scatter.2.cloned.1.call-update) | async-done | bytes 65552 | tf_op jit(solution)/shard_map/reduce_scatter | solution.py:53
  305.6 0.8 sqrt_add_fusion
  306.5 1.5 broadcast_divide_fusion
  308.0 0.6 copy.66
  308.6 0.6 copy.67
  309.2 62.1 %all-gather.2.cloned.1.call-done = f32[2,8,8,4096]{3,1,2,0:T(8,128)} async-done(((f32[2,8,8,128]{3,1,2,0:T(8,128)}), f32[2,8,8,4096]{3,1,2,0:T(8,128)}) %all-gather.2.cloned.1.call-update) | async-done | bytes 2097168 | tf_op jit(solution)/shard_map/all_gather | solution.py:64
  371.3 3.6 convolution_bitcast_fusion.2
  374.9 0.3 copy.64
  375.2 0.4 reshape.80
  375.6 1.9 fusion.12
  377.5 9.1 %broadcast_multiply_fusion = f32[2,16,256,256]{3,2,1,0:T(8,128)} fusion(f32[2,16,64,256]{3,2,1,0:T(8,128)S(1)} %fusion.12, f32[256,64]{0,1:T(8,128)S(1)} %copy-done), kind=kOutput, calls=%fused_computation.13 | convolution fusion | flops 1612709888 | bytes 10551296 | tf_op jit(solution)/shard_map/ia,pmao->pmio/dot_general | solution.py:69
  386.5 8.7 %copy.65 = f32[2,2,8,256,256]{4,3,2,1,0:T(8,128)} copy(f32[2,2,8,256,256]{3,4,2,1,0:T(8,128)} %bitcast.75) | data formatting | bytes 16777216 | tf_op jit(solution)/shard_map/mul | solution.py:71
  395.3 10.6 %sub.18 = f32[2,2,8,256,256]{4,3,2,1,0:T(8,128)} subtract(f32[2,2,8,256,256]{4,3,2,1,0:T(8,128)} %param.10, f32[2,2,8,256,256]{4,3,2,1,0:T(8,128)} %copy.65) | non-fusion elementwise | flops 2097152 | bytes 25165824 | tf_op jit(solution)/shard_map/sub | solution.py:71
  (11 shorter events, 0.1 us)
Async XLA Ops:
  7.2 107.1 %copy-start = (f32[256,64]{0,1:T(8,128)S(1)}, f32[256,64]{0,1:T(8,128)}, u32[]{:S(2)}) copy-start(f32[256,64]{0,1:T(8,128)} %param.12) | copy-start | bytes 196612
  23.0 41.3 %all-to-all-start.1 = ((bf16[2,1,2048,256]{3,0,1,2:T(2,128)(2,1)}), bf16[2,1,2048,256]{3,0,1,2:T(2,128)(2,1)S(1)}, u32[]{:S(2)}, u32[]{:S(2)}) async-start(bf16[2,1,2048,256]{3,0,1,2:T(2,128)(2,1)} %copy.53), calls=%async_computation.1 | async-start | bytes 4194304 | tf_op jit(solution)/shard_map/all_to_all | solution.py:36
  64.3 35.5 %all-to-all-start = ((bf16[2,1,2048,256]{3,0,1,2:T(2,128)(2,1)}), bf16[2,1,2048,256]{3,0,1,2:T(2,128)(2,1)}, u32[]{:S(2)}, u32[]{:S(2)}) async-start(bf16[2,1,2048,256]{3,0,1,2:T(2,128)(2,1)} %copy.50), calls=%async_computation | async-start | bytes 4194304 | tf_op jit(solution)/shard_map/all_to_all | solution.py:39
  70.1 235.5 %reduce-scatter.2.cloned.1.call-start = ((), (), s32[]{:S(2)}) async-start(), calls=%async_computation.3 | async-start | bytes 2162688 | tf_op jit(solution)/shard_map/reduce_scatter | solution.py:53
  107.8 0.8 copy-start.1
  116.3 0.7 copy-start.4
  117.0 188.7 %copy-start.3 = (f32[8,8,128]{2,1,0:T(8,128)S(1)}, f32[8,8,128]{2,1,0:T(8,128)}, u32[]{:S(2)}) copy-start(f32[8,8,128]{2,1,0:T(8,128)} %param.15) | copy-start | bytes 98308
  117.0 189.5 %copy-start.2 = (f32[2,8,8,128]{3,2,1,0:T(8,128)S(1)}, f32[2,8,8,128]{3,2,1,0:T(8,128)}, u32[]{:S(2)}) copy-start(f32[2,8,8,128]{3,2,1,0:T(8,128)} %param.14) | copy-start | bytes 196612
  120.6 250.7 %all-gather.2.cloned.1.call-start = ((), (), s32[]{:S(2)}) async-start(), calls=%async_computation.4 | async-start | bytes 2162688 | tf_op jit(solution)/shard_map/all_gather | solution.py:64
Sparse Core Ops, SparseCore 0:
  120.7 184.9 reduce-scatter.1
  309.0 62.2 all-gather.1
where the time goes:
time: 413 us
  waiting for transfers between devices  291 us (70%)
  local copies, waits for them, and re-layouts  43.2 us (10%)
  matrix products  33 us (8%)
  starting transfers between devices  17.2 us (4%)
  between operations  14.2 us (3%)
  other arithmetic  14.1 us (3%)
    reduce_scatter x1, waiting for transfers between devices, local(): lax.psum_scatter(partial_core, 'wide', scatter_dimension=3, tiled=True)  185 us
    all_gather x1, waiting for transfers between devices, local(): lax.all_gather(core_step, 'wide', axis=3, tiled=True)  62.1 us
    all_to_all x1, waiting for transfers between devices, local(): lax.all_to_all(arrange(out_grads), ('wide', 'narrow'), split_axis=2, conc...  29.5 us
    reshape x2, local copies, waits for them, and re-layouts, arrange(): source.reshape(2, sample_rows, wide_count * narrow_count * local_modes, w...  28 us
    all_to_all x1, waiting for transfers between devices, local(): lax.all_to_all(arrange(spectra), ('wide', 'narrow'), split_axis=2, concat...  14.4 us
    all_to_all x1, starting transfers between devices, local(): lax.all_to_all(arrange(spectra), ('wide', 'narrow'), split_axis=2, concat...  11.2 us
    sub x1, other arithmetic, local(): new_weights = weights - 0.3 * change  10.6 us
    dot_general x1, matrix products, local(): jnp.einsum('ia,pmao->pmio', in_factor, left_part, precision=highest)  9.08 us
  transfers between devices with their start and end apart: 4, of which 4 were waited for; matrix products, arithmetic and copies ran while one was open for 4% of the time, Pallas kernels for 0%

commit v1 on v0

v1 whole, which is shorter than its diff:
```python
import jax
import jax.numpy as jnp
from jax import lax
from jax.experimental import pallas as pl
from jax.experimental.pallas import tpu as pltpu
from jax.sharding import PartitionSpec as P

STEP = 1000
F32 = jnp.float32
BF16 = jnp.bfloat16

GRAD_SCALE = 16.0
FLOOR = 2.0**-12
EDGE = 125.0
SLOPE = 250.0 / 22.2


def encode(v):
    power = jnp.exp2(SLOPE * jnp.log2(1.0 + jnp.abs(v) * (1.0 / FLOOR)) - EDGE)
    return jnp.where(v < 0, -power, power).astype(BF16)


def decode(code):
    y = code.astype(F32)
    size = jnp.exp2((jnp.log2(jnp.abs(y)) + EDGE) * (1.0 / SLOPE)) - 1.0
    return jnp.where(y < 0, -size, size)


def split(v):
    high = v.astype(BF16)
    return high, (v - high.astype(F32)).astype(BF16)


def dot(a, b, dims):
    return lax.dot_general(a, b, (dims, ((), ())), preferred_element_type=F32)


NN = ((1,), (0,))
NT = ((1,), (1,))
TN = ((0,), (0,))


def paired_rows(ref, held):
    half = ref.shape[0] // 2
    for c in range(2):
        held[c] = ref[:, c * 128 : c * 128 + 128]
    return jnp.concatenate(
        [
            jnp.concatenate([held[c, pl.ds(k, half, stride=2), :] for c in range(2)], axis=1)
            for k in range(2)
        ],
        axis=0,
    )


def project_kernel(x_ref, g_ref, in_ref, out_ref, sent_ref, factors, held):
    rows_first = x_ref.shape[1]
    narrow = x_ref.shape[2] // 8

    @pl.when(pl.program_id(0) == 0)
    def _():
        for side, factor in ((0, paired_rows(in_ref, held)), (1, GRAD_SCALE * out_ref[...])):
            high, low = split(factor)
            none = jnp.zeros_like(high)
            factors[2 * side] = jnp.concatenate([high, none, low, none], axis=0)
            factors[2 * side + 1] = jnp.concatenate([none, high, none, low], axis=0)

    for side, ref in ((0, x_ref), (1, g_ref)):
        modes = rows_first * ref.shape[2]
        real = ref[0].reshape(modes, ref.shape[3])
        imag = ref[1].reshape(modes, ref.shape[3])
        both = dot(real, factors[2 * side], NT) + dot(imag, factors[2 * side + 1], NT)
        code = encode(both[:, :128] + both[:, 128:])
        code = code.reshape(rows_first // 2, 2, narrow, 8, 128)
        for w in range(rows_first // 2):
            for n in range(narrow):
                block = jnp.concatenate([code[w, 0, n], code[w, 1, n]], axis=0)
                sent_ref[w * narrow + n, :, side * 128 : side * 128 + 128] = block


def product_kernel(got_ref, core_ref, values):
    samples, modes, lanes = got_ref.shape
    step = 16

    @pl.loop(0, samples // step)
    def _(i):
        block = got_ref[pl.ds(i * step, step)].reshape(step * modes, lanes)
        plain = decode(block)
        for c in range(2):
            values[c, pl.ds(i * step * modes, step * modes), :] = plain[:, c * 128 : c * 128 + 128]

    wide = core_ref.shape[0] // (2 * modes)
    for m in range(modes):
        s_high, s_low = split(values[0, pl.ds(m, samples, stride=modes), :])
        g_high, g_low = split(values[1, pl.ds(m, samples, stride=modes), :])
        left = jnp.concatenate([s_high, s_low], axis=1)
        right = jnp.concatenate([g_high, g_low], axis=1)
        full = dot(left, right, TN)
        core = (full[128:, 128:] + full[:128, 128:]) + full[128:, :128] + full[:128, :128]
        real = core[:64, :64] + core[64:, 64:]
        imag = core[:64, 64:] - core[64:, :64]
        for p, part in ((0, real), (1, imag)):
            tile = jnp.concatenate([part[:32], part[32:]], axis=1) * (FLOOR * FLOOR / GRAD_SCALE)
            core_ref[pl.ds(p * modes + m, wide, stride=2 * modes), :] = tile


def adam_kernel(mode_ref, core_ref, first_ref, second_ref, step_ref, new_first_ref, new_second_ref):
    ranks = mode_ref.shape[0]
    wide = core_ref.shape[0]
    zero = jnp.zeros((8, 128), F32)

    def gather(w, total):
        total = list(total)
        for k in range(2):
            for r in range(ranks):
                factor = mode_ref[r, 2 * w + k]
                for p in range(2):
                    at = p * ranks + r
                    total[at] = total[at] + factor * core_ref[w, pl.ds(16 * p + 8 * k, 8), :]
        return tuple(total)

    total = lax.fori_loop(0, wide, gather, (zero,) * (2 * ranks), unroll=4)
    first_scale = 1.0 / (1.0 - 0.9**STEP)
    second_scale = 1.0 / (1.0 - 0.999**STEP)
    steps = [None] * (2 * ranks)
    for r in range(ranks):
        real, imag = total[r], total[ranks + r]
        second = 0.999 * second_ref[r] + 0.001 * (real * real + imag * imag)
        new_second_ref[r] = second
        below = jnp.sqrt(second * second_scale) + 1e-08
        for p, grad in ((0, real), (1, imag)):
            first = 0.9 * first_ref[p, r] + 0.1 * grad
            new_first_ref[p, r] = first
            steps[p * ranks + r] = first * first_scale / below

    def expand(w, carry):
        for k in range(2):
            parts = [zero, zero]
            for r in range(ranks):
                factor = mode_ref[r, 2 * w + k]
                for p in range(2):
                    parts[p] = parts[p] + factor * steps[p * ranks + r]
            for p in range(2):
                step_ref[w, pl.ds(16 * p + 8 * k, 8), :] = parts[p]
        return carry

    lax.fori_loop(0, wide, expand, 0, unroll=4)


def change_kernel(step_ref, in_ref, out_ref, weights_ref, new_ref, right, left, held):
    count = weights_ref.shape[0]
    wide = step_ref.shape[0] // 32
    at = pl.program_id(0)

    @pl.when(at == 0)
    def _():
        high, low = split(out_ref[...])
        none = jnp.zeros_like(high)
        for half, part in ((0, high), (1, low)):
            right[half, :, :256] = jnp.concatenate([part, none], axis=0)
            right[half, :, 256:] = jnp.concatenate([none, part], axis=0)
        high, low = split(paired_rows(in_ref, held))
        left[...] = jnp.concatenate([high, high, low], axis=0)

    rows = jnp.concatenate(
        [step_ref[pl.ds(at * count + j, wide, stride=32), :] for j in range(count)], axis=0
    )
    high, low = split(rows)
    half = dot(high, right[1], NN) + dot(low, right[0], NN) + dot(high, right[0], NN)
    for j in range(count):
        one = half[j * wide : (j + 1) * wide]
        high, low = split(jnp.concatenate([one[:, :256], one[:, 256:]], axis=0))
        stacked = jnp.concatenate([high, low, high], axis=0)
        new_ref[j] = weights_ref[j] - 0.3 * dot(left[...], stacked, TN)


def whole(*shape):
    return pl.BlockSpec(shape, lambda *_: (0,) * len(shape))


def local(
    spectra, out_grads, weights, mode_factor, in_factor, out_factor, first_moment, second_moment
):
    wide = lax.axis_size("wide")
    narrow = lax.axis_size("narrow")
    _, _, modes_first, modes_second, channels = spectra.shape
    ranks = mode_factor.shape[1]
    modes = (modes_first // wide) * (modes_second // narrow)
    in_rows = in_factor.T
    out_rows = out_factor.T
    mode_rows = mode_factor.T
    parts = 8
    rows_first = modes_first // parts

    source = pl.BlockSpec(
        (2, None, rows_first, modes_second, channels), lambda i: (0, 0, i, 0, 0)
    )
    sent = pl.pallas_call(
        project_kernel,
        grid=(parts,),
        in_specs=[source, source, whole(64, channels), whole(64, channels)],
        out_specs=pl.BlockSpec((wide * narrow // parts, modes, 256), lambda i: (i, 0, 0)),
        out_shape=jax.ShapeDtypeStruct((wide * narrow, modes, 256), BF16),
        scratch_shapes=[pltpu.VMEM((4, 256, channels), BF16), pltpu.VMEM((2, 64, 128), F32)],
        name="project",
    )(spectra, out_grads, in_rows, out_rows)
    got = lax.all_to_all(sent, ("wide", "narrow"), split_axis=0, concat_axis=0, tiled=True)
    samples = got.shape[0]
    core = pl.pallas_call(
        product_kernel,
        out_shape=jax.ShapeDtypeStruct((wide * 2 * modes, 128), F32),
        scratch_shapes=[pltpu.VMEM((2, samples * modes, 128), F32)],
        name="product",
    )(got)
    core = core.reshape(wide, 2 * modes, 128)
    core = lax.all_to_all(core, "wide", split_axis=0, concat_axis=0, tiled=True)
    vmem = pl.BlockSpec(memory_space=pltpu.VMEM)
    step, new_first, new_second = pl.pallas_call(
        adam_kernel,
        in_specs=[pl.BlockSpec(memory_space=pltpu.SMEM), vmem, vmem, vmem],
        out_specs=[vmem, vmem, vmem],
        out_shape=[
            jax.ShapeDtypeStruct(core.shape, F32),
            jax.ShapeDtypeStruct(first_moment.shape, F32),
            jax.ShapeDtypeStruct(second_moment.shape, F32),
        ],
        name="adam",
    )(mode_rows, core, first_moment, second_moment)
    step = lax.all_to_all(step, "wide", split_axis=0, concat_axis=0, tiled=True)
    flat = weights.reshape(2 * modes, channels, channels)
    count = 4
    block = pl.BlockSpec((count, channels, channels), lambda i: (i, 0, 0))
    new_weights = pl.pallas_call(
        change_kernel,
        grid=(2 * modes // count,),
        in_specs=[whole(wide * 2 * modes, 128), whole(64, channels), whole(64, channels), block],
        out_specs=block,
        out_shape=jax.ShapeDtypeStruct(flat.shape, F32),
        scratch_shapes=[
            pltpu.VMEM((2, 128, 512), BF16),
            pltpu.VMEM((192, channels), BF16),
            pltpu.VMEM((2, 64, 128), F32),
        ],
        name="change",
    )(step.reshape(wide * 2 * modes, 128), in_rows, out_rows, flat)
    return (new_weights.reshape(weights.shape), new_first, new_second)


def solution(mesh):
    placed = (
        P(None, ("wide", "narrow"), None, None, None),
        P(None, ("wide", "narrow"), None, None, None),
        P(None, "wide", "narrow", None, None),
        P(),
        P(),
        P(),
        P(None, None, "narrow", "wide"),
        P(None, "narrow", "wide"),
    )
    return jax.shard_map(
        local,
        mesh=mesh,
        in_specs=placed,
        out_specs=(
            P(None, "wide", "narrow", None, None),
            P(None, None, "narrow", "wide"),
            P(None, "narrow", "wide"),
        ),
        check_vma=False,
    )
```

time: 413 us -> 92 us (0.22)
  waiting for transfers between devices: 291 us -> 0 us
  blocking collectives: 0 us -> 64.7 us
  local copies, waits for them, and re-layouts: 43.2 us -> 0 us
  matrix products: 33 us -> 0 us
  Pallas kernels: 0 us -> 25.9 us
  starting transfers between devices: 17.2 us -> 0 us
  other arithmetic: 14.1 us -> 0 us
  between operations: 14.2 us -> 0.63 us
    reduce_scatter x1 -> x0, waiting for transfers between devices: 185 us -> none  [local(): lax.psum_scatter(partial_core, 'wide', scatter_dimension=3, tiled=True)]
    all_to_all x0 -> x3, blocking collectives: none -> 64.7 us  [the longest x1 30.1 us: local(): lax.all_to_all(sent, ('wide', 'narrow'), split_axis=0, concat_axis=0, til...]
    all_gather x1 -> x0, waiting for transfers between devices: 62.1 us -> none  [local(): lax.all_gather(core_step, 'wide', axis=3, tiled=True)]
    all_to_all x2 -> x0, waiting for transfers between devices: 43.8 us -> none  [the longest x1 29.5 us: local(): lax.all_to_all(arrange(out_grads), ('wide', 'narrow'), split_axis=2, conc...]
    dot_general x7 -> x0, matrix products: 33 us -> none  [the longest x1 9.08 us: local(): jnp.einsum('ia,pmao->pmio', in_factor, left_part, precision=highest)]
    reshape x4 -> x0, local copies, waits for them, and re-layouts: 28.8 us -> none  [the longest x2 28 us: arrange(): source.reshape(2, sample_rows, wide_count * narrow_count * local_modes, w...]
    pallas_call x0 -> x4, Pallas kernels: none -> 25.9 us  [the longest x1 10.9 us: local(): pl.pallas_call(change_kernel, grid=(2 * modes // count,), in_specs=[whole...]
    all_to_all x2 -> x0, starting transfers between devices: 17 us -> none  [the longest x1 11.2 us: local(): lax.all_to_all(arrange(spectra), ('wide', 'narrow'), split_axis=2, concat...]
  transfers between devices with their start and end apart: 4 -> 0, of which waited for: 4 -> 0; matrix products, arithmetic and copies ran while one was open for 4% -> 0% of each run, Pallas kernels for 0% -> 0%
where the time goes in v1:
time: 92 us; the launch traced here: 91.2 us
  blocking collectives  64.7 us (70%)
  Pallas kernels  25.9 us (28%)
    all_to_all x1, blocking collectives, local(): lax.all_to_all(sent, ('wide', 'narrow'), split_axis=0, concat_axis=0, til...  30.1 us
    all_to_all x1, blocking collectives, local(): core = lax.all_to_all(core, 'wide', split_axis=0, concat_axis=0, tiled=True)  18.1 us
    all_to_all x1, blocking collectives, local(): step = lax.all_to_all(step, 'wide', split_axis=0, concat_axis=0, tiled=True)  16.5 us
    pallas_call x1, Pallas kernels, local(): pl.pallas_call(change_kernel, grid=(2 * modes // count,), in_specs=[whole...  10.9 us
    pallas_call x1, Pallas kernels, local(): pl.pallas_call(project_kernel, grid=(parts,), in_specs=[source, source, w...  7.33 us
    pallas_call x1, Pallas kernels, local(): pl.pallas_call(product_kernel, out_shape=jax.ShapeDtypeStruct((wide * 2 *...  4.77 us
    pallas_call x1, Pallas kernels, local(): pl.pallas_call(adam_kernel, in_specs=[pl.BlockSpec(memory_space=pltpu.SME...  2.98 us

profile of v1, /device:TPU:0, one launch (start us, length us, event | category | flops | bytes accessed | tf_op | source)
XLA Modules:
  0.0 91.2 jit_solution(9787883895223549379)
XLA Ops:
  0.6 7.3 %project.1 = bf16[128,16,256]{2,1,0:T(8,128)(2,1)} custom-call(bf16[2,1,64,32,256]{4,3,2,1,0:T(8,128)(2,1)} %x_ref.1, bf16[2,1,64,32,256]{4,3,2,1,0:T(8,128)(2,1)} %g_ref.1, f32[64,256]{1,0:T(8,128)} %bitcast.11, f32[64,256]{1,0:T(8,128)} %bitcast.13), custom_call_target="tpu_custom_call" | custom-call | tf_op jit(solution)/shard_map/project/pallas_call | solution.py:198
  8.0 30.1 %all_to_all.15.got_ref = bf16[128,16,256]{2,1,0:T(8,128)(2,1)} all-to-all(bf16[128,16,256]{2,1,0:T(8,128)(2,1)} %project.1), channel_id=1, replica_groups=mesh['wide'=32,'narrow'=4] {'wide','narrow'}, dimensions={0} | all-to-all | bytes 2097152 | tf_op jit(solution)/shard_map/all_to_all | solution.py:207
  38.1 4.8 %product.1 = f32[1024,128]{1,0:T(8,128)} custom-call(bf16[128,16,256]{2,1,0:T(8,128)(2,1)} %all_to_all.15.got_ref), custom_call_target="tpu_custom_call" | custom-call | tf_op jit(solution)/shard_map/product/pallas_call | solution.py:209
  42.8 18.1 %all_to_all.16.core_ref = f32[32,32,128]{2,1,0:T(8,128)} all-to-all(f32[32,32,128]{2,1,0:T(8,128)} %bitcast.9), channel_id=1, replica_groups=mesh['wide'=32,'narrow'=4] {'wide'}, dimensions={0} | all-to-all | bytes 1048576 | tf_op jit(solution)/shard_map/all_to_all | solution.py:216
  60.9 3.0 %adam.1 = (f32[32,32,128]{2,1,0:T(8,128)}, f32[2,8,8,128]{3,2,1,0:T(8,128)}, f32[8,8,128]{2,1,0:T(8,128)}) custom-call(f32[8,64]{1,0:T(8,128)} %bitcast.15, f32[32,32,128]{2,1,0:T(8,128)} %all_to_all.16.core_ref, f32[2,8,8,128]{3,2,1,0:T(8,128)} %first_ref.1, f32[8,8,128]{2,1,0:T(8,128)} %second_ref.1), custom_call_target="tpu_custom_call" | custom-call | tf_op jit(solution)/shard_map/adam/pallas_call | solution.py:218
  63.9 16.5 %all_to_all.17 = f32[32,32,128]{2,1,0:T(8,128)} all-to-all(f32[32,32,128]{2,1,0:T(8,128)} %get-tuple-element.6), channel_id=1, replica_groups=mesh['wide'=32,'narrow'=4] {'wide'}, dimensions={0} | all-to-all | bytes 1048576 | tf_op jit(solution)/shard_map/all_to_all | solution.py:229
  80.4 10.9 %change.1 = f32[32,256,256]{2,1,0:T(8,128)} custom-call(f32[1024,128]{1,0:T(8,128)} %bitcast.10, f32[64,256]{1,0:T(8,128)} %bitcast.12, f32[64,256]{1,0:T(8,128)} %bitcast.14, f32[32,256,256]{2,1,0:T(8,128)} %bitcast.7), custom_call_target="tpu_custom_call" | custom-call | tf_op jit(solution)/shard_map/change/pallas_call | solution.py:233

commit v2 on v1

--- a/solution.py
+++ b/solution.py
@@ -36,7 +36,6 @@
 
 
 NN = ((1,), (0,))
-NT = ((1,), (1,))
 TN = ((0,), (0,))
 
 
@@ -53,29 +52,58 @@
     )
 
 
-def project_kernel(x_ref, g_ref, in_ref, out_ref, sent_ref, factors, held):
-    rows_first = x_ref.shape[1]
-    narrow = x_ref.shape[2] // 8
-
-    @pl.when(pl.program_id(0) == 0)
-    def _():
-        for side, factor in ((0, paired_rows(in_ref, held)), (1, GRAD_SCALE * out_ref[...])):
-            high, low = split(factor)
-            none = jnp.zeros_like(high)
-            factors[2 * side] = jnp.concatenate([high, none, low, none], axis=0)
-            factors[2 * side + 1] = jnp.concatenate([none, high, none, low], axis=0)
-
-    for side, ref in ((0, x_ref), (1, g_ref)):
-        modes = rows_first * ref.shape[2]
-        real = ref[0].reshape(modes, ref.shape[3])
-        imag = ref[1].reshape(modes, ref.shape[3])
-        both = dot(real, factors[2 * side], NT) + dot(imag, factors[2 * side + 1], NT)
-        code = encode(both[:, :128] + both[:, 128:])
-        code = code.reshape(rows_first // 2, 2, narrow, 8, 128)
-        for w in range(rows_first // 2):
-            for n in range(narrow):
-                block = jnp.concatenate([code[w, 0, n], code[w, 1, n]], axis=0)
-                sent_ref[w * narrow + n, :, side * 128 : side * 128 + 128] = block
+def project_kernel(
+    x_hbm, g_hbm, in_hbm_ref, out_hbm_ref, sent_ref, sources, rows, factors, held, sems, row_sems
+):
+    parts = sems.shape[1]
+    rows_first = sources.shape[2] // parts
+    modes_second, channels = sources.shape[3:]
+    narrow = modes_second // 8
+    modes = rows_first * modes_second
+
+    def fetch(side, i):
+        at = pl.ds(i * rows_first, rows_first)
+        hbm = (x_hbm, g_hbm)[side]
+        return pltpu.make_async_copy(hbm.at[:, 0, at], sources.at[side, :, at], sems.at[side, i])
+
+    def fetch_rows(side):
+        hbm = (in_hbm_ref, out_hbm_ref)[side]
+        return pltpu.make_async_copy(hbm, rows.at[side], row_sems.at[side])
+
+    for side in range(2):
+        fetch_rows(side).start()
+    ahead = 1
+    for i in range(ahead):
+        for side in range(2):
+            fetch(side, i).start()
+    for side in range(2):
+        fetch_rows(side).wait()
+        factor = GRAD_SCALE * rows[1] if side else paired_rows(rows.at[0], held)
+        high, low = split(factor)
+        none = jnp.zeros_like(high)
+        factors[2 * side] = jnp.concatenate([high, none, low, none], axis=0).T
+        factors[2 * side + 1] = jnp.concatenate([none, high, none, low], axis=0).T
+
+    @pl.loop(0, parts)
+    def _(i):
+        for side in range(2):
+            fetch(side, i).wait()
+
+            @pl.when(i + ahead < parts)
+            def _():
+                fetch(side, i + ahead).start()
+
+            at = pl.ds(i * rows_first, rows_first)
+            real = sources[side, 0, at].reshape(modes, channels)
+            imag = sources[side, 1, at].reshape(modes, channels)
+            both = dot(real, factors[2 * side], NN) + dot(imag, factors[2 * side + 1], NN)
+            code = encode(both[:, :128] + both[:, 128:])
+            code = code.reshape(rows_first // 2, 2, narrow, 8, 128)
+            for w in range(rows_first // 2):
+                for n in range(narrow):
+                    block = jnp.concatenate([code[w, 0, n], code[w, 1, n]], axis=0)
+                    dest = i * (rows_first // 2 * narrow) + w * narrow + n
+                    sent_ref[dest, :, side * 128 : side * 128 + 128] = block
 
 
 def product_kernel(got_ref, core_ref, values):
@@ -104,7 +132,18 @@
             core_ref[pl.ds(p * modes + m, wide, stride=2 * modes), :] = tile
 
 
-def adam_kernel(mode_ref, core_ref, first_ref, second_ref, step_ref, new_first_ref, new_second_ref):
+def adam_kernel(
+    mode_ref,
+    core_ref,
+    first_ref,
+    second_ref,
+    step_ref,
+    first_hbm,
+    second_hbm,
+    new_first_ref,
+    new_second_ref,
+    sems,
+):
     ranks = mode_ref.shape[0]
     wide = core_ref.shape[0]
     zero = jnp.zeros((8, 128), F32)
@@ -133,6 +172,13 @@
             new_first_ref[p, r] = first
             steps[p * ranks + r] = first * first_scale / below
 
+    copies = [
+        pltpu.make_async_copy(new_first_ref, first_hbm, sems.at[0]),
+        pltpu.make_async_copy(new_second_ref, second_hbm, sems.at[1]),
+    ]
+    for copy in copies:
+        copy.start()
+
     def expand(w, carry):
         for k in range(2):
             parts = [zero, zero]
@@ -145,37 +191,49 @@
         return carry
 
     lax.fori_loop(0, wide, expand, 0, unroll=4)
-
-
-def change_kernel(step_ref, in_ref, out_ref, weights_ref, new_ref, right, left, held):
-    count = weights_ref.shape[0]
-    wide = step_ref.shape[0] // 32
-    at = pl.program_id(0)
-
-    @pl.when(at == 0)
-    def _():
-        high, low = split(out_ref[...])
-        none = jnp.zeros_like(high)
-        for half, part in ((0, high), (1, low)):
-            right[half, :, :256] = jnp.concatenate([part, none], axis=0)
-            right[half, :, 256:] = jnp.concatenate([none, part], axis=0)
-        high, low = split(paired_rows(in_ref, held))
-        left[...] = jnp.concatenate([high, high, low], axis=0)
-
-    rows = jnp.concatenate(
-        [step_ref[pl.ds(at * count + j, wide, stride=32), :] for j in range(count)], axis=0
-    )
-    high, low = split(rows)
-    half = dot(high, right[1], NN) + dot(low, right[0], NN) + dot(high, right[0], NN)
-    for j in range(count):
-        one = half[j * wide : (j + 1) * wide]
-        high, low = split(jnp.concatenate([one[:, :256], one[:, 256:]], axis=0))
-        stacked = jnp.concatenate([high, low, high], axis=0)
-        new_ref[j] = weights_ref[j] - 0.3 * dot(left[...], stacked, TN)
-
-
-def whole(*shape):
-    return pl.BlockSpec(shape, lambda *_: (0,) * len(shape))
+    for copy in copies:
+        copy.wait()
+
+
+def change_kernel(
+    step_ref, in_ref, out_ref, weights_ref, new_hbm, right, left, held, changed, sems
+):
+    modes = weights_ref.shape[0]
+    wide = step_ref.shape[0] // modes
+    count = 8
+    high, low = split(out_ref[...])
+    none = jnp.zeros_like(high)
+    for half, part in ((0, high), (1, low)):
+        right[half, :, :256] = jnp.concatenate([part, none], axis=0)
+        right[half, :, 256:] = jnp.concatenate([none, part], axis=0)
+    high, low = split(0.3 * paired_rows(in_ref, held))
+    left[...] = jnp.concatenate([high, high, low], axis=0).T
+
+    def give(m):
+        return pltpu.make_async_copy(changed.at[m], new_hbm.at[m], sems.at[m])
+
+    @pl.loop(0, modes // count)
+    def _(i):
+        rows = jnp.concatenate(
+            [step_ref[pl.ds(i * count + j, wide, stride=modes), :] for j in range(count)], axis=0
+        )
+        high, low = split(rows)
+        half = dot(high, right[1], NN) + dot(low, right[0], NN) + dot(high, right[0], NN)
+        for j in range(count):
+            m = i * count + j
+            one = half[j * wide : (j + 1) * wide]
+            high, low = split(jnp.concatenate([one[:, :256], one[:, 256:]], axis=0))
+            stacked = jnp.concatenate([high, low, high], axis=0)
+            changed[m] = weights_ref[m] - dot(left[...], stacked, NN)
+            give(m).start()
+
+    @pl.loop(0, modes)
+    def _(m):
+        give(m).wait()
+
+
+def in_hbm(array):
+    return pltpu.with_memory_space_constraint(array, pltpu.HBM)
 
 
 def local(
@@ -189,21 +247,25 @@
     in_rows = in_factor.T
     out_rows = out_factor.T
     mode_rows = mode_factor.T
-    parts = 8
-    rows_first = modes_first // parts
-
-    source = pl.BlockSpec(
-        (2, None, rows_first, modes_second, channels), lambda i: (0, 0, i, 0, 0)
-    )
+    parts = 2
+    vmem = pl.BlockSpec(memory_space=pltpu.VMEM)
+    hbm = pl.BlockSpec(memory_space=pl.ANY)
     sent = pl.pallas_call(
         project_kernel,
-        grid=(parts,),
-        in_specs=[source, source, whole(64, channels), whole(64, channels)],
-        out_specs=pl.BlockSpec((wide * narrow // parts, modes, 256), lambda i: (i, 0, 0)),
+        in_specs=[hbm] * 4,
+        out_specs=vmem,
         out_shape=jax.ShapeDtypeStruct((wide * narrow, modes, 256), BF16),
-        scratch_shapes=[pltpu.VMEM((4, 256, channels), BF16), pltpu.VMEM((2, 64, 128), F32)],
+        scratch_shapes=[
+            pltpu.VMEM((2, 2, modes_first, modes_second, channels), BF16),
+            pltpu.VMEM((2, 64, channels), F32),
+            pltpu.VMEM((4, channels, 256), BF16),
+            pltpu.VMEM((2, 64, 128), F32),
+            pltpu.SemaphoreType.DMA((2, parts)),
+            pltpu.SemaphoreType.DMA((2,)),
+        ],
         name="project",
-    )(spectra, out_grads, in_rows, out_rows)
+        compiler_params=pltpu.CompilerParams(vmem_limit_bytes=12 * 2**20),
+    )(in_hbm(spectra), in_hbm(out_grads), in_hbm(in_rows), in_hbm(out_rows))
     got = lax.all_to_all(sent, ("wide", "narrow"), split_axis=0, concat_axis=0, tiled=True)
     samples = got.shape[0]
     core = pl.pallas_call(
@@ -211,37 +273,43 @@
         out_shape=jax.ShapeDtypeStruct((wide * 2 * modes, 128), F32),
         scratch_shapes=[pltpu.VMEM((2, samples * modes, 128), F32)],
         name="product",
+        compiler_params=pltpu.CompilerParams(vmem_limit_bytes=8 * 2**20),
     )(got)
     core = core.reshape(wide, 2 * modes, 128)
     core = lax.all_to_all(core, "wide", split_axis=0, concat_axis=0, tiled=True)
-    vmem = pl.BlockSpec(memory_space=pltpu.VMEM)
     step, new_first, new_second = pl.pallas_call(
         adam_kernel,
         in_specs=[pl.BlockSpec(memory_space=pltpu.SMEM), vmem, vmem, vmem],
-        out_specs=[vmem, vmem, vmem],
+        out_specs=[vmem, hbm, hbm],
         out_shape=[
             jax.ShapeDtypeStruct(core.shape, F32),
             jax.ShapeDtypeStruct(first_moment.shape, F32),
             jax.ShapeDtypeStruct(second_moment.shape, F32),
         ],
+        scratch_shapes=[
+            pltpu.VMEM(first_moment.shape, F32),
+            pltpu.VMEM(second_moment.shape, F32),
+            pltpu.SemaphoreType.DMA((2,)),
+        ],
         name="adam",
+        compiler_params=pltpu.CompilerParams(vmem_limit_bytes=4 * 2**20),
     )(mode_rows, core, first_moment, second_moment)
     step = lax.all_to_all(step, "wide", split_axis=0, concat_axis=0, tiled=True)
     flat = weights.reshape(2 * modes, channels, channels)
-    count = 4
-    block = pl.BlockSpec((count, channels, channels), lambda i: (i, 0, 0))
     new_weights = pl.pallas_call(
         change_kernel,
-        grid=(2 * modes // count,),
-        in_specs=[whole(wide * 2 * modes, 128), whole(64, channels), whole(64, channels), block],
-        out_specs=block,
+        in_specs=[vmem] * 4,
+        out_specs=hbm,
         out_shape=jax.ShapeDtypeStruct(flat.shape, F32),
         scratch_shapes=[
             pltpu.VMEM((2, 128, 512), BF16),
-            pltpu.VMEM((192, channels), BF16),
+            pltpu.VMEM((channels, 192), BF16),
             pltpu.VMEM((2, 64, 128), F32),
+            pltpu.VMEM(flat.shape, F32),
+            pltpu.SemaphoreType.DMA((2 * modes,)),
         ],
         name="change",
+        compiler_params=pltpu.CompilerParams(vmem_limit_bytes=12 * 2**20),
     )(step.reshape(wide * 2 * modes, 128), in_rows, out_rows, flat)
     return (new_weights.reshape(weights.shape), new_first, new_second)
 

time: 92 us -> 77.7 us (0.84)
  Pallas kernels: 25.9 us -> 13.6 us
  blocking collectives: 64.7 us -> 63.2 us
    pallas_call x2, Pallas kernels: 18.2 us -> 9.02 us  [the longest x1 4.58 us: local(): pl.pallas_call(change_kernel, in_specs=[vmem] * 4, out_specs=hbm, out_sha...]
    pallas_call x1, Pallas kernels: 4.77 us -> 2.76 us  [local(): pl.pallas_call(product_kernel, out_shape=jax.ShapeDtypeStruct((wide * 2 *...]
    pallas_call x1, Pallas kernels: 2.98 us -> 1.79 us  [local(): pl.pallas_call(adam_kernel, in_specs=[pl.BlockSpec(memory_space=pltpu.SME...]
where the time goes in v2:
time: 77.7 us; the launch traced here: 77.5 us
  blocking collectives  63.2 us (81%)
  Pallas kernels  13.6 us (18%)
    all_to_all x1, blocking collectives, local(): lax.all_to_all(sent, ('wide', 'narrow'), split_axis=0, concat_axis=0, til...  29.8 us
    all_to_all x1, blocking collectives, local(): core = lax.all_to_all(core, 'wide', split_axis=0, concat_axis=0, tiled=True)  17.3 us
    all_to_all x1, blocking collectives, local(): step = lax.all_to_all(step, 'wide', split_axis=0, concat_axis=0, tiled=True)  16.2 us
    pallas_call x1, Pallas kernels, local(): pl.pallas_call(change_kernel, in_specs=[vmem] * 4, out_specs=hbm, out_sha...  4.58 us
    pallas_call x1, Pallas kernels, local(): pl.pallas_call(project_kernel, in_specs=[hbm] * 4, out_specs=vmem, out_sh...  4.44 us
    pallas_call x1, Pallas kernels, local(): pl.pallas_call(product_kernel, out_shape=jax.ShapeDtypeStruct((wide * 2 *...  2.76 us
    pallas_call x1, Pallas kernels, local(): pl.pallas_call(adam_kernel, in_specs=[pl.BlockSpec(memory_space=pltpu.SME...  1.79 us

profile of v2, /device:TPU:0, one launch (start us, length us, event | category | flops | bytes accessed | tf_op | source)
XLA Modules:
  0.0 77.5 jit_solution(3218655583437255569)
XLA Ops:
  0.6 0.0 copy-start.2
  0.6 0.0 copy-start.1
  0.7 0.0 copy-start.4
  0.7 0.0 copy-start.3
  0.7 0.0 copy-start.5
  0.7 0.0 copy-start
  0.7 4.4 %project.1 = bf16[128,16,256]{2,1,0:T(8,128)(2,1)S(1)} custom-call(bf16[2,1,64,32,256]{4,3,2,1,0:T(8,128)(2,1)} %x_hbm.1, bf16[2,1,64,32,256]{4,3,2,1,0:T(8,128)(2,1)} %g_hbm.1, f32[64,256]{1,0:T(8,128)} %bitcast.10, f32[64,256]{1,0:T(8,128)} %bitcast.12), custom_call_target="tpu_custom_call" | custom-call | tf_op jit(solution)/shard_map/project/pallas_call | solution.py:253
  5.1 29.8 %all_to_all.15.got_ref = bf16[128,16,256]{2,1,0:T(8,128)(2,1)S(1)} all-to-all(bf16[128,16,256]{2,1,0:T(8,128)(2,1)S(1)} %project.1), channel_id=1, replica_groups=mesh['wide'=32,'narrow'=4] {'wide','narrow'}, dimensions={0} | all-to-all | bytes 2097152 | tf_op jit(solution)/shard_map/all_to_all | solution.py:269
  34.9 2.8 %product.1 = f32[1024,128]{1,0:T(8,128)S(1)} custom-call(bf16[128,16,256]{2,1,0:T(8,128)(2,1)S(1)} %all_to_all.15.got_ref), custom_call_target="tpu_custom_call" | custom-call | tf_op jit(solution)/shard_map/product/pallas_call | solution.py:271
  37.7 17.3 %all_to_all.16.core_ref = f32[32,32,128]{2,1,0:T(8,128)S(1)} all-to-all(f32[32,32,128]{2,1,0:T(8,128)S(1)} %bitcast.8), channel_id=1, replica_groups=mesh['wide'=32,'narrow'=4] {'wide'}, dimensions={0} | all-to-all | bytes 1048576 | tf_op jit(solution)/shard_map/all_to_all | solution.py:279
  55.0 0.0 copy-done.4
  55.0 0.0 copy-done.3
  55.0 0.0 copy-done.5
  55.0 1.8 %adam.1 = (f32[32,32,128]{2,1,0:T(8,128)S(1)}, f32[2,8,8,128]{3,2,1,0:T(8,128)}, f32[8,8,128]{2,1,0:T(8,128)}) custom-call(f32[8,64]{1,0:T(8,128)S(1)} %bitcast.14, f32[32,32,128]{2,1,0:T(8,128)S(1)} %all_to_all.16.core_ref, f32[2,8,8,128]{3,2,1,0:T(8,128)S(1)} %copy-done.3, f32[8,8,128]{2,1,0:T(8,128)S(1)} %copy-done.4), custom_call_target="tpu_custom_call" | custom-call | tf_op jit(solution)/shard_map/adam/pallas_call | solution.py:280
  56.8 16.2 %all_to_all.17 = f32[32,32,128]{2,1,0:T(8,128)S(1)} all-to-all(f32[32,32,128]{2,1,0:T(8,128)S(1)} %get-tuple-element.6), channel_id=1, replica_groups=mesh['wide'=32,'narrow'=4] {'wide'}, dimensions={0} | all-to-all | bytes 1048576 | tf_op jit(solution)/shard_map/all_to_all | solution.py:297
  72.9 0.0 copy-done.2
  72.9 0.0 copy-done.1
  72.9 0.0 copy-done
  72.9 4.6 %change.1 = f32[32,256,256]{2,1,0:T(8,128)} custom-call(f32[1024,128]{1,0:T(8,128)S(1)} %bitcast.9, f32[64,256]{1,0:T(8,128)S(1)} %bitcast.11, f32[64,256]{1,0:T(8,128)S(1)} %bitcast.13, f32[32,256,256]{2,1,0:T(8,128)S(1)} %bitcast.7), custom_call_target="tpu_custom_call" | custom-call | tf_op jit(solution)/shard_map/change/pallas_call | solution.py:299
Async XLA Ops:
  0.6 72.3 %copy-start.2 = (f32[256,64]{0,1:T(8,128)S(1)}, f32[256,64]{0,1:T(8,128)}, u32[]{:S(2)}) copy-start(f32[256,64]{0,1:T(8,128)} %param.13) | copy-start | bytes 196612
  0.6 72.3 %copy-start.1 = (f32[256,64]{0,1:T(8,128)S(1)}, f32[256,64]{0,1:T(8,128)}, u32[]{:S(2)}) copy-start(f32[256,64]{0,1:T(8,128)} %param.12) | copy-start | bytes 196612
  0.7 54.3 %copy-start.4 = (f32[8,8,128]{2,1,0:T(8,128)S(1)}, f32[8,8,128]{2,1,0:T(8,128)}, u32[]{:S(2)}) copy-start(f32[8,8,128]{2,1,0:T(8,128)} %second_ref.1) | copy-start | bytes 98308
  0.7 54.3 %copy-start.3 = (f32[2,8,8,128]{3,2,1,0:T(8,128)S(1)}, f32[2,8,8,128]{3,2,1,0:T(8,128)}, u32[]{:S(2)}) copy-start(f32[2,8,8,128]{3,2,1,0:T(8,128)} %first_ref.1) | copy-start | bytes 196612
  0.7 54.3 %copy-start.5 = (f32[64,8]{0,1:T(8,128)S(1)}, f32[64,8]{0,1:T(8,128)}, u32[]{:S(2)}) copy-start(f32[64,8]{0,1:T(8,128)} %param.11) | copy-start | bytes 6148
  0.7 72.3 %copy-start = (f32[2,2,8,256,256]{4,3,2,1,0:T(8,128)S(1)}, f32[2,2,8,256,256]{4,3,2,1,0:T(8,128)}, u32[]{:S(2)}) copy-start(f32[2,2,8,256,256]{4,3,2,1,0:T(8,128)} %param.10) | copy-start | bytes 25165828

commit v3 on v2

--- a/solution.py
+++ b/solution.py
@@ -20,8 +20,7 @@
     return jnp.where(v < 0, -power, power).astype(BF16)
 
 
-def decode(code):
-    y = code.astype(F32)
+def decode(y):
     size = jnp.exp2((jnp.log2(jnp.abs(y)) + EDGE) * (1.0 / SLOPE)) - 1.0
     return jnp.where(y < 0, -size, size)
 
@@ -113,14 +112,14 @@
     @pl.loop(0, samples // step)
     def _(i):
         block = got_ref[pl.ds(i * step, step)].reshape(step * modes, lanes)
-        plain = decode(block)
+        plain = block.astype(F32)
         for c in range(2):
             values[c, pl.ds(i * step * modes, step * modes), :] = plain[:, c * 128 : c * 128 + 128]
 
     wide = core_ref.shape[0] // (2 * modes)
     for m in range(modes):
-        s_high, s_low = split(values[0, pl.ds(m, samples, stride=modes), :])
-        g_high, g_low = split(values[1, pl.ds(m, samples, stride=modes), :])
+        s_high, s_low = split(decode(values[0, pl.ds(m, samples, stride=modes), :]))
+        g_high, g_low = split(decode(values[1, pl.ds(m, samples, stride=modes), :]))
         left = jnp.concatenate([s_high, s_low], axis=1)
         right = jnp.concatenate([g_high, g_low], axis=1)
         full = dot(left, right, TN)
@@ -200,7 +199,7 @@
 ):
     modes = weights_ref.shape[0]
     wide = step_ref.shape[0] // modes
-    count = 8
+    count = 16
     high, low = split(out_ref[...])
     none = jnp.zeros_like(high)
     for half, part in ((0, high), (1, low)):
@@ -309,7 +308,7 @@
             pltpu.SemaphoreType.DMA((2 * modes,)),
         ],
         name="change",
-        compiler_params=pltpu.CompilerParams(vmem_limit_bytes=12 * 2**20),
+        compiler_params=pltpu.CompilerParams(vmem_limit_bytes=14 * 2**20),
     )(step.reshape(wide * 2 * modes, 128), in_rows, out_rows, flat)
     return (new_weights.reshape(weights.shape), new_first, new_second)
 

time: 77.7 us -> 77.2 us (level)
  no operation moved by 1% of the time
where the time goes in v3:
time: 77.2 us; the launch traced here: 77 us
  blocking collectives  63.2 us (82%)
  Pallas kernels  13 us (17%)
    all_to_all x1, blocking collectives, local(): lax.all_to_all(sent, ('wide', 'narrow'), split_axis=0, concat_axis=0, til...  29.8 us
    all_to_all x1, blocking collectives, local(): core = lax.all_to_all(core, 'wide', split_axis=0, concat_axis=0, tiled=True)  17.3 us
    all_to_all x1, blocking collectives, local(): step = lax.all_to_all(step, 'wide', split_axis=0, concat_axis=0, tiled=True)  16.2 us
    pallas_call x1, Pallas kernels, local(): pl.pallas_call(project_kernel, in_specs=[hbm] * 4, out_specs=vmem, out_sh...  4.44 us
    pallas_call x1, Pallas kernels, local(): pl.pallas_call(change_kernel, in_specs=[vmem] * 4, out_specs=hbm, out_sha...  4.31 us
    pallas_call x1, Pallas kernels, local(): pl.pallas_call(product_kernel, out_shape=jax.ShapeDtypeStruct((wide * 2 *...  2.48 us
    pallas_call x1, Pallas kernels, local(): pl.pallas_call(adam_kernel, in_specs=[pl.BlockSpec(memory_space=pltpu.SME...  1.79 us

profile of v3, /device:TPU:0, one launch (start us, length us, event | category | flops | bytes accessed | tf_op | source)
XLA Modules:
  0.0 77.0 jit_solution(5245268608442508639)
XLA Ops:
  0.6 0.0 copy-start.2
  0.6 0.0 copy-start.1
  0.7 0.0 copy-start.4
  0.7 0.0 copy-start.3
  0.7 0.0 copy-start.5
  0.7 0.0 copy-start
  0.7 4.4 %project.1 = bf16[128,16,256]{2,1,0:T(8,128)(2,1)S(1)} custom-call(bf16[2,1,64,32,256]{4,3,2,1,0:T(8,128)(2,1)} %x_hbm.1, bf16[2,1,64,32,256]{4,3,2,1,0:T(8,128)(2,1)} %g_hbm.1, f32[64,256]{1,0:T(8,128)} %bitcast.10, f32[64,256]{1,0:T(8,128)} %bitcast.12), custom_call_target="tpu_custom_call" | custom-call | tf_op jit(solution)/shard_map/project/pallas_call | solution.py:252
  5.1 29.8 %all_to_all.15.got_ref = bf16[128,16,256]{2,1,0:T(8,128)(2,1)S(1)} all-to-all(bf16[128,16,256]{2,1,0:T(8,128)(2,1)S(1)} %project.1), channel_id=1, replica_groups=mesh['wide'=32,'narrow'=4] {'wide','narrow'}, dimensions={0} | all-to-all | bytes 2097152 | tf_op jit(solution)/shard_map/all_to_all | solution.py:268
  34.9 2.5 %product.1 = f32[1024,128]{1,0:T(8,128)S(1)} custom-call(bf16[128,16,256]{2,1,0:T(8,128)(2,1)S(1)} %all_to_all.15.got_ref), custom_call_target="tpu_custom_call" | custom-call | tf_op jit(solution)/shard_map/product/pallas_call | solution.py:270
  37.4 17.3 %all_to_all.16.core_ref = f32[32,32,128]{2,1,0:T(8,128)S(1)} all-to-all(f32[32,32,128]{2,1,0:T(8,128)S(1)} %bitcast.8), channel_id=1, replica_groups=mesh['wide'=32,'narrow'=4] {'wide'}, dimensions={0} | all-to-all | bytes 1048576 | tf_op jit(solution)/shard_map/all_to_all | solution.py:278
  54.7 0.0 copy-done.4
  54.7 0.0 copy-done.3
  54.7 0.0 copy-done.5
  54.7 1.8 %adam.1 = (f32[32,32,128]{2,1,0:T(8,128)S(1)}, f32[2,8,8,128]{3,2,1,0:T(8,128)}, f32[8,8,128]{2,1,0:T(8,128)}) custom-call(f32[8,64]{1,0:T(8,128)S(1)} %bitcast.14, f32[32,32,128]{2,1,0:T(8,128)S(1)} %all_to_all.16.core_ref, f32[2,8,8,128]{3,2,1,0:T(8,128)S(1)} %copy-done.3, f32[8,8,128]{2,1,0:T(8,128)S(1)} %copy-done.4), custom_call_target="tpu_custom_call" | custom-call | tf_op jit(solution)/shard_map/adam/pallas_call | solution.py:279
  56.5 16.2 %all_to_all.17 = f32[32,32,128]{2,1,0:T(8,128)S(1)} all-to-all(f32[32,32,128]{2,1,0:T(8,128)S(1)} %get-tuple-element.6), channel_id=1, replica_groups=mesh['wide'=32,'narrow'=4] {'wide'}, dimensions={0} | all-to-all | bytes 1048576 | tf_op jit(solution)/shard_map/all_to_all | solution.py:296
  72.6 0.0 copy-done.2
  72.6 0.0 copy-done.1
  72.6 0.0 copy-done
  72.7 4.3 %change.1 = f32[32,256,256]{2,1,0:T(8,128)} custom-call(f32[1024,128]{1,0:T(8,128)S(1)} %bitcast.9, f32[64,256]{1,0:T(8,128)S(1)} %bitcast.11, f32[64,256]{1,0:T(8,128)S(1)} %bitcast.13, f32[32,256,256]{2,1,0:T(8,128)S(1)} %bitcast.7), custom_call_target="tpu_custom_call" | custom-call | tf_op jit(solution)/shard_map/change/pallas_call | solution.py:298
Async XLA Ops:
  0.6 72.0 %copy-start.2 = (f32[256,64]{0,1:T(8,128)S(1)}, f32[256,64]{0,1:T(8,128)}, u32[]{:S(2)}) copy-start(f32[256,64]{0,1:T(8,128)} %param.13) | copy-start | bytes 196612
  0.6 72.0 %copy-start.1 = (f32[256,64]{0,1:T(8,128)S(1)}, f32[256,64]{0,1:T(8,128)}, u32[]{:S(2)}) copy-start(f32[256,64]{0,1:T(8,128)} %param.12) | copy-start | bytes 196612
  0.7 54.0 %copy-start.4 = (f32[8,8,128]{2,1,0:T(8,128)S(1)}, f32[8,8,128]{2,1,0:T(8,128)}, u32[]{:S(2)}) copy-start(f32[8,8,128]{2,1,0:T(8,128)} %second_ref.1) | copy-start | bytes 98308
  0.7 54.0 %copy-start.3 = (f32[2,8,8,128]{3,2,1,0:T(8,128)S(1)}, f32[2,8,8,128]{3,2,1,0:T(8,128)}, u32[]{:S(2)}) copy-start(f32[2,8,8,128]{3,2,1,0:T(8,128)} %first_ref.1) | copy-start | bytes 196612
  0.7 54.0 %copy-start.5 = (f32[64,8]{0,1:T(8,128)S(1)}, f32[64,8]{0,1:T(8,128)}, u32[]{:S(2)}) copy-start(f32[64,8]{0,1:T(8,128)} %param.11) | copy-start | bytes 6148
  0.7 72.0 %copy-start = (f32[2,2,8,256,256]{4,3,2,1,0:T(8,128)S(1)}, f32[2,2,8,256,256]{4,3,2,1,0:T(8,128)}, u32[]{:S(2)}) copy-start(f32[2,2,8,256,256]{4,3,2,1,0:T(8,128)} %param.10) | copy-start | bytes 25165828

commit v4 on v3

--- a/solution.py
+++ b/solution.py
@@ -202,9 +202,8 @@
     count = 16
     high, low = split(out_ref[...])
     none = jnp.zeros_like(high)
-    for half, part in ((0, high), (1, low)):
-        right[half, :, :256] = jnp.concatenate([part, none], axis=0)
-        right[half, :, 256:] = jnp.concatenate([none, part], axis=0)
+    right[0] = jnp.concatenate([high, high, low, none], axis=0)
+    right[1] = jnp.concatenate([high, high, none, low], axis=0)
     high, low = split(0.3 * paired_rows(in_ref, held))
     left[...] = jnp.concatenate([high, high, low], axis=0).T
 
@@ -216,12 +215,21 @@
         rows = jnp.concatenate(
             [step_ref[pl.ds(i * count + j, wide, stride=modes), :] for j in range(count)], axis=0
         )
-        high, low = split(rows)
-        half = dot(high, right[1], NN) + dot(low, right[0], NN) + dot(high, right[0], NN)
+        high, _ = split(rows)
+        coarse = high.astype(F32)
+        turned = pltpu.roll(rows - coarse, 64, 1)
+        first_half = lax.broadcasted_iota(jnp.int32, rows.shape, 1) < 64
+        even, odd = (
+            dot(jnp.concatenate([mixed.astype(BF16), high], axis=1), right[k], NN)
+            for k, mixed in (
+                (0, jnp.where(first_half, coarse, turned)),
+                (1, jnp.where(first_half, turned, coarse)),
+            )
+        )
         for j in range(count):
             m = i * count + j
-            one = half[j * wide : (j + 1) * wide]
-            high, low = split(jnp.concatenate([one[:, :256], one[:, 256:]], axis=0))
+            mine = slice(j * wide, (j + 1) * wide)
+            high, low = split(jnp.concatenate([even[mine], odd[mine]], axis=0))
             stacked = jnp.concatenate([high, low, high], axis=0)
             changed[m] = weights_ref[m] - dot(left[...], stacked, NN)
             give(m).start()
@@ -301,7 +309,7 @@
         out_specs=hbm,
         out_shape=jax.ShapeDtypeStruct(flat.shape, F32),
         scratch_shapes=[
-            pltpu.VMEM((2, 128, 512), BF16),
+            pltpu.VMEM((2, 256, channels), BF16),
             pltpu.VMEM((channels, 192), BF16),
             pltpu.VMEM((2, 64, 128), F32),
             pltpu.VMEM(flat.shape, F32),

time: 77.2 us -> 77 us (level)
  no operation moved by 1% of the time
where the time goes in v4:
time: 77 us; the launch traced here: 76.8 us
  blocking collectives  63.2 us (82%)
  Pallas kernels  12.8 us (17%)
    all_to_all x1, blocking collectives, local(): lax.all_to_all(sent, ('wide', 'narrow'), split_axis=0, concat_axis=0, til...  29.8 us
    all_to_all x1, blocking collectives, local(): core = lax.all_to_all(core, 'wide', split_axis=0, concat_axis=0, tiled=True)  17.3 us
    all_to_all x1, blocking collectives, local(): step = lax.all_to_all(step, 'wide', split_axis=0, concat_axis=0, tiled=True)  16.2 us
    pallas_call x1, Pallas kernels, local(): pl.pallas_call(project_kernel, in_specs=[hbm] * 4, out_specs=vmem, out_sh...  4.44 us
    pallas_call x1, Pallas kernels, local(): pl.pallas_call(change_kernel, in_specs=[vmem] * 4, out_specs=hbm, out_sha...  4.1 us
    pallas_call x1, Pallas kernels, local(): pl.pallas_call(product_kernel, out_shape=jax.ShapeDtypeStruct((wide * 2 *...  2.48 us
    pallas_call x1, Pallas kernels, local(): pl.pallas_call(adam_kernel, in_specs=[pl.BlockSpec(memory_space=pltpu.SME...  1.79 us

profile of v4, /device:TPU:0, one launch (start us, length us, event | category | flops | bytes accessed | tf_op | source)
XLA Modules:
  0.0 76.8 jit_solution(9145540616902705323)
XLA Ops:
  0.6 0.0 copy-start.2
  0.6 0.0 copy-start.1
  0.7 0.0 copy-start.4
  0.7 0.0 copy-start.3
  0.7 0.0 copy-start.5
  0.7 0.0 copy-start
  0.7 4.4 %project.1 = bf16[128,16,256]{2,1,0:T(8,128)(2,1)S(1)} custom-call(bf16[2,1,64,32,256]{4,3,2,1,0:T(8,128)(2,1)} %x_hbm.1, bf16[2,1,64,32,256]{4,3,2,1,0:T(8,128)(2,1)} %g_hbm.1, f32[64,256]{1,0:T(8,128)} %bitcast.10, f32[64,256]{1,0:T(8,128)} %bitcast.12), custom_call_target="tpu_custom_call" | custom-call | tf_op jit(solution)/shard_map/project/pallas_call | solution.py:260
  5.1 29.8 %all_to_all.15.got_ref = bf16[128,16,256]{2,1,0:T(8,128)(2,1)S(1)} all-to-all(bf16[128,16,256]{2,1,0:T(8,128)(2,1)S(1)} %project.1), channel_id=1, replica_groups=mesh['wide'=32,'narrow'=4] {'wide','narrow'}, dimensions={0} | all-to-all | bytes 2097152 | tf_op jit(solution)/shard_map/all_to_all | solution.py:276
  34.9 2.5 %product.1 = f32[1024,128]{1,0:T(8,128)S(1)} custom-call(bf16[128,16,256]{2,1,0:T(8,128)(2,1)S(1)} %all_to_all.15.got_ref), custom_call_target="tpu_custom_call" | custom-call | tf_op jit(solution)/shard_map/product/pallas_call | solution.py:278
  37.4 17.3 %all_to_all.16.core_ref = f32[32,32,128]{2,1,0:T(8,128)S(1)} all-to-all(f32[32,32,128]{2,1,0:T(8,128)S(1)} %bitcast.8), channel_id=1, replica_groups=mesh['wide'=32,'narrow'=4] {'wide'}, dimensions={0} | all-to-all | bytes 1048576 | tf_op jit(solution)/shard_map/all_to_all | solution.py:286
  54.7 0.0 copy-done.4
  54.7 0.0 copy-done.3
  54.7 0.0 copy-done.5
  54.7 1.8 %adam.1 = (f32[32,32,128]{2,1,0:T(8,128)S(1)}, f32[2,8,8,128]{3,2,1,0:T(8,128)}, f32[8,8,128]{2,1,0:T(8,128)}) custom-call(f32[8,64]{1,0:T(8,128)S(1)} %bitcast.14, f32[32,32,128]{2,1,0:T(8,128)S(1)} %all_to_all.16.core_ref, f32[2,8,8,128]{3,2,1,0:T(8,128)S(1)} %copy-done.3, f32[8,8,128]{2,1,0:T(8,128)S(1)} %copy-done.4), custom_call_target="tpu_custom_call" | custom-call | tf_op jit(solution)/shard_map/adam/pallas_call | solution.py:287
  56.5 16.2 %all_to_all.17 = f32[32,32,128]{2,1,0:T(8,128)S(1)} all-to-all(f32[32,32,128]{2,1,0:T(8,128)S(1)} %get-tuple-element.6), channel_id=1, replica_groups=mesh['wide'=32,'narrow'=4] {'wide'}, dimensions={0} | all-to-all | bytes 1048576 | tf_op jit(solution)/shard_map/all_to_all | solution.py:304
  72.6 0.0 copy-done.2
  72.6 0.0 copy-done.1
  72.6 0.0 copy-done
  72.7 4.1 %change.1 = f32[32,256,256]{2,1,0:T(8,128)} custom-call(f32[1024,128]{1,0:T(8,128)S(1)} %bitcast.9, f32[64,256]{1,0:T(8,128)S(1)} %bitcast.11, f32[64,256]{1,0:T(8,128)S(1)} %bitcast.13, f32[32,256,256]{2,1,0:T(8,128)S(1)} %bitcast.7), custom_call_target="tpu_custom_call" | custom-call | tf_op jit(solution)/shard_map/change/pallas_call | solution.py:306
Async XLA Ops:
  0.6 72.0 %copy-start.2 = (f32[256,64]{0,1:T(8,128)S(1)}, f32[256,64]{0,1:T(8,128)}, u32[]{:S(2)}) copy-start(f32[256,64]{0,1:T(8,128)} %param.13) | copy-start | bytes 196612
  0.6 72.0 %copy-start.1 = (f32[256,64]{0,1:T(8,128)S(1)}, f32[256,64]{0,1:T(8,128)}, u32[]{:S(2)}) copy-start(f32[256,64]{0,1:T(8,128)} %param.12) | copy-start | bytes 196612
  0.7 54.0 %copy-start.4 = (f32[8,8,128]{2,1,0:T(8,128)S(1)}, f32[8,8,128]{2,1,0:T(8,128)}, u32[]{:S(2)}) copy-start(f32[8,8,128]{2,1,0:T(8,128)} %second_ref.1) | copy-start | bytes 98308
  0.7 54.0 %copy-start.3 = (f32[2,8,8,128]{3,2,1,0:T(8,128)S(1)}, f32[2,8,8,128]{3,2,1,0:T(8,128)}, u32[]{:S(2)}) copy-start(f32[2,8,8,128]{3,2,1,0:T(8,128)} %first_ref.1) | copy-start | bytes 196612
  0.7 54.0 %copy-start.5 = (f32[64,8]{0,1:T(8,128)S(1)}, f32[64,8]{0,1:T(8,128)}, u32[]{:S(2)}) copy-start(f32[64,8]{0,1:T(8,128)} %param.11) | copy-start | bytes 6148
  0.7 72.0 %copy-start = (f32[2,2,8,256,256]{4,3,2,1,0:T(8,128)S(1)}, f32[2,2,8,256,256]{4,3,2,1,0:T(8,128)}, u32[]{:S(2)}) copy-start(f32[2,2,8,256,256]{4,3,2,1,0:T(8,128)} %param.10) | copy-start | bytes 25165828

commit v5 on v4

--- a/solution.py
+++ b/solution.py
@@ -58,7 +58,6 @@
     rows_first = sources.shape[2] // parts
     modes_second, channels = sources.shape[3:]
     narrow = modes_second // 8
-    modes = rows_first * modes_second
 
     def fetch(side, i):
         at = pl.ds(i * rows_first, rows_first)
@@ -71,10 +70,8 @@
 
     for side in range(2):
         fetch_rows(side).start()
-    ahead = 1
-    for i in range(ahead):
-        for side in range(2):
-            fetch(side, i).start()
+    for i in range(parts):
+        fetch(0, i).start()
     for side in range(2):
         fetch_rows(side).wait()
         factor = GRAD_SCALE * rows[1] if side else paired_rows(rows.at[0], held)
@@ -83,26 +80,32 @@
         factors[2 * side] = jnp.concatenate([high, none, low, none], axis=0).T
         factors[2 * side + 1] = jnp.concatenate([none, high, none, low], axis=0).T
 
+    def emit(side, at, count, base):
+        modes = count * modes_second
+        real = sources[side, 0, at].reshape(modes, channels)
+        imag = sources[side, 1, at].reshape(modes, channels)
+        both = dot(real, factors[2 * side], NN) + dot(imag, factors[2 * side + 1], NN)
+        code = encode(both[:, :128] + both[:, 128:])
+        code = code.reshape(count // 2, 2, narrow, 8, 128)
+        for w in range(count // 2):
+            for n in range(narrow):
+                block = jnp.concatenate([code[w, 0, n], code[w, 1, n]], axis=0)
+                sent_ref[base + w * narrow + n, :, side * 128 : side * 128 + 128] = block
+
     @pl.loop(0, parts)
     def _(i):
-        for side in range(2):
-            fetch(side, i).wait()
-
-            @pl.when(i + ahead < parts)
-            def _():
-                fetch(side, i + ahead).start()
-
-            at = pl.ds(i * rows_first, rows_first)
-            real = sources[side, 0, at].reshape(modes, channels)
-            imag = sources[side, 1, at].reshape(modes, channels)
-            both = dot(real, factors[2 * side], NN) + dot(imag, factors[2 * side + 1], NN)
-            code = encode(both[:, :128] + both[:, 128:])
-            code = code.reshape(rows_first // 2, 2, narrow, 8, 128)
-            for w in range(rows_first // 2):
-                for n in range(narrow):
-                    block = jnp.concatenate([code[w, 0, n], code[w, 1, n]], axis=0)
-                    dest = i * (rows_first // 2 * narrow) + w * narrow + n
-                    sent_ref[dest, :, side * 128 : side * 128 + 128] = block
+        fetch(0, i).wait()
+
+        @pl.when(i == 0)
+        def _():
+            for k in range(parts):
+                fetch(1, k).start()
+
+        emit(0, pl.ds(i * rows_first, rows_first), rows_first, i * (rows_first // 2 * narrow))
+
+    for k in range(parts):
+        fetch(1, k).wait()
+    emit(1, slice(None), parts * rows_first, 0)
 
 
 def product_kernel(got_ref, core_ref, values):

time: 77 us -> 76.6 us (level)
  no operation moved by 1% of the time
where the time goes in v5:
time: 76.6 us; the launch traced here: 76.4 us
  blocking collectives  63.2 us (83%)
  Pallas kernels  12.4 us (16%)
    all_to_all x1, blocking collectives, local(): lax.all_to_all(sent, ('wide', 'narrow'), split_axis=0, concat_axis=0, til...  29.8 us
    all_to_all x1, blocking collectives, local(): core = lax.all_to_all(core, 'wide', split_axis=0, concat_axis=0, tiled=True)  17.2 us
    all_to_all x1, blocking collectives, local(): step = lax.all_to_all(step, 'wide', split_axis=0, concat_axis=0, tiled=True)  16.2 us
    pallas_call x1, Pallas kernels, local(): pl.pallas_call(change_kernel, in_specs=[vmem] * 4, out_specs=hbm, out_sha...  4.1 us
    pallas_call x1, Pallas kernels, local(): pl.pallas_call(project_kernel, in_specs=[hbm] * 4, out_specs=vmem, out_sh...  4.06 us
    pallas_call x1, Pallas kernels, local(): pl.pallas_call(product_kernel, out_shape=jax.ShapeDtypeStruct((wide * 2 *...  2.48 us
    pallas_call x1, Pallas kernels, local(): pl.pallas_call(adam_kernel, in_specs=[pl.BlockSpec(memory_space=pltpu.SME...  1.79 us

profile of v5, /device:TPU:0, one launch (start us, length us, event | category | flops | bytes accessed | tf_op | source)
XLA Modules:
  0.0 76.4 jit_solution(3822747875186273181)
XLA Ops:
  0.6 0.0 copy-start.2
  0.6 0.0 copy-start.1
  0.7 0.0 copy-start.4
  0.7 0.0 copy-start.3
  0.7 0.0 copy-start.5
  0.7 0.0 copy-start
  0.7 4.1 %project.1 = bf16[128,16,256]{2,1,0:T(8,128)(2,1)S(1)} custom-call(bf16[2,1,64,32,256]{4,3,2,1,0:T(8,128)(2,1)} %x_hbm.1, bf16[2,1,64,32,256]{4,3,2,1,0:T(8,128)(2,1)} %g_hbm.1, f32[64,256]{1,0:T(8,128)} %bitcast.10, f32[64,256]{1,0:T(8,128)} %bitcast.12), custom_call_target="tpu_custom_call" | custom-call | tf_op jit(solution)/shard_map/project/pallas_call | solution.py:263
  4.8 29.8 %all_to_all.15.got_ref = bf16[128,16,256]{2,1,0:T(8,128)(2,1)S(1)} all-to-all(bf16[128,16,256]{2,1,0:T(8,128)(2,1)S(1)} %project.1), channel_id=1, replica_groups=mesh['wide'=32,'narrow'=4] {'wide','narrow'}, dimensions={0} | all-to-all | bytes 2097152 | tf_op jit(solution)/shard_map/all_to_all | solution.py:279
  34.6 2.5 %product.1 = f32[1024,128]{1,0:T(8,128)S(1)} custom-call(bf16[128,16,256]{2,1,0:T(8,128)(2,1)S(1)} %all_to_all.15.got_ref), custom_call_target="tpu_custom_call" | custom-call | tf_op jit(solution)/shard_map/product/pallas_call | solution.py:281
  37.0 17.2 %all_to_all.16.core_ref = f32[32,32,128]{2,1,0:T(8,128)S(1)} all-to-all(f32[32,32,128]{2,1,0:T(8,128)S(1)} %bitcast.8), channel_id=1, replica_groups=mesh['wide'=32,'narrow'=4] {'wide'}, dimensions={0} | all-to-all | bytes 1048576 | tf_op jit(solution)/shard_map/all_to_all | solution.py:289
  54.3 0.0 copy-done.4
  54.3 0.0 copy-done.3
  54.3 0.0 copy-done.5
  54.3 1.8 %adam.1 = (f32[32,32,128]{2,1,0:T(8,128)S(1)}, f32[2,8,8,128]{3,2,1,0:T(8,128)}, f32[8,8,128]{2,1,0:T(8,128)}) custom-call(f32[8,64]{1,0:T(8,128)S(1)} %bitcast.14, f32[32,32,128]{2,1,0:T(8,128)S(1)} %all_to_all.16.core_ref, f32[2,8,8,128]{3,2,1,0:T(8,128)S(1)} %copy-done.3, f32[8,8,128]{2,1,0:T(8,128)S(1)} %copy-done.4), custom_call_target="tpu_custom_call" | custom-call | tf_op jit(solution)/shard_map/adam/pallas_call | solution.py:290
  56.1 16.2 %all_to_all.17 = f32[32,32,128]{2,1,0:T(8,128)S(1)} all-to-all(f32[32,32,128]{2,1,0:T(8,128)S(1)} %get-tuple-element.6), channel_id=1, replica_groups=mesh['wide'=32,'narrow'=4] {'wide'}, dimensions={0} | all-to-all | bytes 1048576 | tf_op jit(solution)/shard_map/all_to_all | solution.py:307
  72.3 0.0 copy-done.2
  72.3 0.0 copy-done.1
  72.3 0.0 copy-done
  72.3 4.1 %change.1 = f32[32,256,256]{2,1,0:T(8,128)} custom-call(f32[1024,128]{1,0:T(8,128)S(1)} %bitcast.9, f32[64,256]{1,0:T(8,128)S(1)} %bitcast.11, f32[64,256]{1,0:T(8,128)S(1)} %bitcast.13, f32[32,256,256]{2,1,0:T(8,128)S(1)} %bitcast.7), custom_call_target="tpu_custom_call" | custom-call | tf_op jit(solution)/shard_map/change/pallas_call | solution.py:309
Async XLA Ops:
  0.6 71.6 %copy-start.2 = (f32[256,64]{0,1:T(8,128)S(1)}, f32[256,64]{0,1:T(8,128)}, u32[]{:S(2)}) copy-start(f32[256,64]{0,1:T(8,128)} %param.13) | copy-start | bytes 196612
  0.6 71.6 %copy-start.1 = (f32[256,64]{0,1:T(8,128)S(1)}, f32[256,64]{0,1:T(8,128)}, u32[]{:S(2)}) copy-start(f32[256,64]{0,1:T(8,128)} %param.12) | copy-start | bytes 196612
  0.7 53.6 %copy-start.4 = (f32[8,8,128]{2,1,0:T(8,128)S(1)}, f32[8,8,128]{2,1,0:T(8,128)}, u32[]{:S(2)}) copy-start(f32[8,8,128]{2,1,0:T(8,128)} %second_ref.1) | copy-start | bytes 98308
  0.7 53.6 %copy-start.3 = (f32[2,8,8,128]{3,2,1,0:T(8,128)S(1)}, f32[2,8,8,128]{3,2,1,0:T(8,128)}, u32[]{:S(2)}) copy-start(f32[2,8,8,128]{3,2,1,0:T(8,128)} %first_ref.1) | copy-start | bytes 196612
  0.7 53.6 %copy-start.5 = (f32[64,8]{0,1:T(8,128)S(1)}, f32[64,8]{0,1:T(8,128)}, u32[]{:S(2)}) copy-start(f32[64,8]{0,1:T(8,128)} %param.11) | copy-start | bytes 6148
  0.7 71.6 %copy-start = (f32[2,2,8,256,256]{4,3,2,1,0:T(8,128)S(1)}, f32[2,2,8,256,256]{4,3,2,1,0:T(8,128)}, u32[]{:S(2)}) copy-start(f32[2,2,8,256,256]{4,3,2,1,0:T(8,128)} %param.10) | copy-start | bytes 25165828

commit v6 on v5

--- a/solution.py
+++ b/solution.py
@@ -211,7 +211,8 @@
     left[...] = jnp.concatenate([high, high, low], axis=0).T
 
     def give(m):
-        return pltpu.make_async_copy(changed.at[m], new_hbm.at[m], sems.at[m])
+        at = pl.ds(2 * m, 2)
+        return pltpu.make_async_copy(changed.at[at], new_hbm.at[at], sems.at[m])
 
     @pl.loop(0, modes // count)
     def _(i):
@@ -235,9 +236,10 @@
             high, low = split(jnp.concatenate([even[mine], odd[mine]], axis=0))
             stacked = jnp.concatenate([high, low, high], axis=0)
             changed[m] = weights_ref[m] - dot(left[...], stacked, NN)
-            give(m).start()
-
-    @pl.loop(0, modes)
+            if j % 2:
+                give(i * (count // 2) + j // 2).start()
+
+    @pl.loop(0, modes // 2)
     def _(m):
         give(m).wait()
 
@@ -316,7 +318,7 @@
             pltpu.VMEM((channels, 192), BF16),
             pltpu.VMEM((2, 64, 128), F32),
             pltpu.VMEM(flat.shape, F32),
-            pltpu.SemaphoreType.DMA((2 * modes,)),
+            pltpu.SemaphoreType.DMA((modes,)),
         ],
         name="change",
         compiler_params=pltpu.CompilerParams(vmem_limit_bytes=14 * 2**20),

time: 76.6 us -> 76.4 us (level)
  no operation moved by 1% of the time
where the time goes in v6:
time: 76.4 us; the launch traced here: 76.2 us
  blocking collectives  63.2 us (83%)
  Pallas kernels  12.3 us (16%)
    all_to_all x1, blocking collectives, local(): lax.all_to_all(sent, ('wide', 'narrow'), split_axis=0, concat_axis=0, til...  29.8 us
    all_to_all x1, blocking collectives, local(): core = lax.all_to_all(core, 'wide', split_axis=0, concat_axis=0, tiled=True)  17.2 us
    all_to_all x1, blocking collectives, local(): step = lax.all_to_all(step, 'wide', split_axis=0, concat_axis=0, tiled=True)  16.2 us
    pallas_call x1, Pallas kernels, local(): pl.pallas_call(project_kernel, in_specs=[hbm] * 4, out_specs=vmem, out_sh...  4.06 us
    pallas_call x1, Pallas kernels, local(): pl.pallas_call(change_kernel, in_specs=[vmem] * 4, out_specs=hbm, out_sha...  3.98 us
    pallas_call x1, Pallas kernels, local(): pl.pallas_call(product_kernel, out_shape=jax.ShapeDtypeStruct((wide * 2 *...  2.48 us
    pallas_call x1, Pallas kernels, local(): pl.pallas_call(adam_kernel, in_specs=[pl.BlockSpec(memory_space=pltpu.SME...  1.79 us

profile of v6, /device:TPU:0, one launch (start us, length us, event | category | flops | bytes accessed | tf_op | source)
XLA Modules:
  0.0 76.2 jit_solution(7459023375358086036)
XLA Ops:
  0.6 0.0 copy-start.2
  0.6 0.0 copy-start.1
  0.7 0.0 copy-start.4
  0.7 0.0 copy-start.3
  0.7 0.0 copy-start.5
  0.7 0.0 copy-start
  0.7 4.1 %project.1 = bf16[128,16,256]{2,1,0:T(8,128)(2,1)S(1)} custom-call(bf16[2,1,64,32,256]{4,3,2,1,0:T(8,128)(2,1)} %x_hbm.1, bf16[2,1,64,32,256]{4,3,2,1,0:T(8,128)(2,1)} %g_hbm.1, f32[64,256]{1,0:T(8,128)} %bitcast.10, f32[64,256]{1,0:T(8,128)} %bitcast.12), custom_call_target="tpu_custom_call" | custom-call | tf_op jit(solution)/shard_map/project/pallas_call | solution.py:265
  4.8 29.8 %all_to_all.15.got_ref = bf16[128,16,256]{2,1,0:T(8,128)(2,1)S(1)} all-to-all(bf16[128,16,256]{2,1,0:T(8,128)(2,1)S(1)} %project.1), channel_id=1, replica_groups=mesh['wide'=32,'narrow'=4] {'wide','narrow'}, dimensions={0} | all-to-all | bytes 2097152 | tf_op jit(solution)/shard_map/all_to_all | solution.py:281
  34.6 2.5 %product.1 = f32[1024,128]{1,0:T(8,128)S(1)} custom-call(bf16[128,16,256]{2,1,0:T(8,128)(2,1)S(1)} %all_to_all.15.got_ref), custom_call_target="tpu_custom_call" | custom-call | tf_op jit(solution)/shard_map/product/pallas_call | solution.py:283
  37.0 17.2 %all_to_all.16.core_ref = f32[32,32,128]{2,1,0:T(8,128)S(1)} all-to-all(f32[32,32,128]{2,1,0:T(8,128)S(1)} %bitcast.8), channel_id=1, replica_groups=mesh['wide'=32,'narrow'=4] {'wide'}, dimensions={0} | all-to-all | bytes 1048576 | tf_op jit(solution)/shard_map/all_to_all | solution.py:291
  54.3 0.0 copy-done.4
  54.3 0.0 copy-done.3
  54.3 0.0 copy-done.5
  54.3 1.8 %adam.1 = (f32[32,32,128]{2,1,0:T(8,128)S(1)}, f32[2,8,8,128]{3,2,1,0:T(8,128)}, f32[8,8,128]{2,1,0:T(8,128)}) custom-call(f32[8,64]{1,0:T(8,128)S(1)} %bitcast.14, f32[32,32,128]{2,1,0:T(8,128)S(1)} %all_to_all.16.core_ref, f32[2,8,8,128]{3,2,1,0:T(8,128)S(1)} %copy-done.3, f32[8,8,128]{2,1,0:T(8,128)S(1)} %copy-done.4), custom_call_target="tpu_custom_call" | custom-call | tf_op jit(solution)/shard_map/adam/pallas_call | solution.py:292
  56.1 16.2 %all_to_all.17 = f32[32,32,128]{2,1,0:T(8,128)S(1)} all-to-all(f32[32,32,128]{2,1,0:T(8,128)S(1)} %get-tuple-element.6), channel_id=1, replica_groups=mesh['wide'=32,'narrow'=4] {'wide'}, dimensions={0} | all-to-all | bytes 1048576 | tf_op jit(solution)/shard_map/all_to_all | solution.py:309
  72.3 0.0 copy-done.2
  72.3 0.0 copy-done.1
  72.3 0.0 copy-done
  72.3 4.0 %change.1 = f32[32,256,256]{2,1,0:T(8,128)} custom-call(f32[1024,128]{1,0:T(8,128)S(1)} %bitcast.9, f32[64,256]{1,0:T(8,128)S(1)} %bitcast.11, f32[64,256]{1,0:T(8,128)S(1)} %bitcast.13, f32[32,256,256]{2,1,0:T(8,128)S(1)} %bitcast.7), custom_call_target="tpu_custom_call" | custom-call | tf_op jit(solution)/shard_map/change/pallas_call | solution.py:311
Async XLA Ops:
  0.6 71.6 %copy-start.2 = (f32[256,64]{0,1:T(8,128)S(1)}, f32[256,64]{0,1:T(8,128)}, u32[]{:S(2)}) copy-start(f32[256,64]{0,1:T(8,128)} %param.13) | copy-start | bytes 196612
  0.6 71.6 %copy-start.1 = (f32[256,64]{0,1:T(8,128)S(1)}, f32[256,64]{0,1:T(8,128)}, u32[]{:S(2)}) copy-start(f32[256,64]{0,1:T(8,128)} %param.12) | copy-start | bytes 196612
  0.7 53.6 %copy-start.4 = (f32[8,8,128]{2,1,0:T(8,128)S(1)}, f32[8,8,128]{2,1,0:T(8,128)}, u32[]{:S(2)}) copy-start(f32[8,8,128]{2,1,0:T(8,128)} %second_ref.1) | copy-start | bytes 98308
  0.7 53.6 %copy-start.3 = (f32[2,8,8,128]{3,2,1,0:T(8,128)S(1)}, f32[2,8,8,128]{3,2,1,0:T(8,128)}, u32[]{:S(2)}) copy-start(f32[2,8,8,128]{3,2,1,0:T(8,128)} %first_ref.1) | copy-start | bytes 196612
  0.7 53.6 %copy-start.5 = (f32[64,8]{0,1:T(8,128)S(1)}, f32[64,8]{0,1:T(8,128)}, u32[]{:S(2)}) copy-start(f32[64,8]{0,1:T(8,128)} %param.11) | copy-start | bytes 6148
  0.7 71.6 %copy-start = (f32[2,2,8,256,256]{4,3,2,1,0:T(8,128)S(1)}, f32[2,2,8,256,256]{4,3,2,1,0:T(8,128)}, u32[]{:S(2)}) copy-start(f32[2,2,8,256,256]{4,3,2,1,0:T(8,128)} %param.10) | copy-start | bytes 25165828
